TPU v7x, 512 devices: a whole 4x8x8 slice. The times are simulated.
512 devices in a mesh: req: 128 (over y, z, core), tp: 4 (over x).
Axes of the slice: x: 4, y: 8, z: 8, core: 2. Of those that a mesh axis runs over, the one named last changes fastest.
Arguments:
- hidden: bfloat16 [1024, 4096], P('req'), may hold values from -512 to 512
- norm_gain: bfloat16 [4096], replicated, may hold values from 1 to 3
- lm_head: bfloat16 [4096, 131072], P(None, ('req', 'tp'))
- targets: int32 [1024], P('req'), may hold values from 0 to 131071
- segments: int32 [1024], P('req'), may hold values from 0 to 3, never falling along the last dimension, each value on 1 to 512 neighbouring positions
- scored: int32 [1024], P('req'), may hold values from 0 to 1, as said below
Outputs:
- token_logprob: float32 [1024], P('req')
- token_entropy: float32 [1024], P('req')
- seq_logprob: float32 [4], replicated
Inputs may be any that keep to these rules, and one draw needn't show every extreme that they name: At most 4 of the 8 rows of one index of req are scored, and exactly 4 on some index in every draw.
All inputs are finite; a program needn't handle non-finite values.
Results may differ from a plain program's by a relative error of at most 0.0061.
Values may be sent and summed in bfloat16 or wider, within the bound.
A program may use at most 64 MiB of HBM per device.

v0:
```python
import jax
import jax.numpy as jnp
from jax import lax
from jax.sharding import PartitionSpec as P

SEQS = 4
SCORE_MOST = 4


def local(hidden, norm_gain, lm_head, targets, segments, scored):
    col_width = lm_head.shape[1]
    own_index = lax.axis_index("req")
    first_col = (own_index * lax.axis_size("tp") + lax.axis_index("tp")) * col_width
    rank = jnp.cumsum(scored) - 1
    slots = jnp.arange(SCORE_MOST, dtype=jnp.int32)
    chosen = (scored[None, :] == 1) & (rank[None, :] == slots[:, None])
    values = jnp.sum(
        jnp.where(chosen[:, :, None], hidden.astype(jnp.float32)[None, :, :], 0.0), axis=1
    )
    row_scale = lax.rsqrt(jnp.mean(values * values, axis=1, keepdims=True) + 1e-05)
    normed = (values * row_scale * norm_gain.astype(jnp.float32)[None, :]).astype(jnp.bfloat16)
    codes = jnp.sum(jnp.where(chosen, (targets * SEQS + segments + 1)[None, :], 0), axis=1) - 1
    rows, row_codes = lax.all_gather((normed, codes), "req", axis=0, tiled=True)
    used = row_codes >= 0
    row_targets = row_codes // SEQS
    row_segments = row_codes % SEQS
    logits = jnp.dot(rows, lm_head, preferred_element_type=jnp.float32)
    own_top = jnp.max(logits, axis=1)
    scaled = jnp.exp(logits - own_top[:, None])
    own_total = jnp.sum(scaled, axis=1)
    own_weighted = jnp.sum(scaled * logits, axis=1)
    columns = first_col + jnp.arange(col_width, dtype=jnp.int32)
    own_picked = jnp.sum(jnp.where(columns[None, :] == row_targets[:, None], logits, 0.0), axis=1)
    row_top = lax.pmax(own_top, ("req", "tp"))
    factor = jnp.exp(own_top - row_top)
    sums = lax.psum(jnp.stack([own_total * factor, own_weighted * factor, own_picked]), ("req", "tp"))
    log_norm = row_top + jnp.log(sums[0])
    logprob = jnp.where(used, sums[2] - log_norm, 0.0)
    entropy = jnp.where(used, log_norm - sums[1] / sums[0], 0.0)
    seq_ids = jnp.arange(SEQS, dtype=jnp.int32)
    seq_logprob = jnp.sum(
        jnp.where(row_segments[None, :] == seq_ids[:, None], logprob[None, :], 0.0), axis=1
    )
    own = own_index * SCORE_MOST
    own_logprob = lax.dynamic_slice_in_dim(logprob, own, SCORE_MOST, 0)
    own_entropy = lax.dynamic_slice_in_dim(entropy, own, SCORE_MOST, 0)
    token_logprob = jnp.sum(jnp.where(chosen, own_logprob[:, None], 0.0), axis=0)
    token_entropy = jnp.sum(jnp.where(chosen, own_entropy[:, None], 0.0), axis=0)
    return (token_logprob, token_entropy, seq_logprob)


def solution(mesh):
    return jax.shard_map(
        local,
        mesh=mesh,
        in_specs=(P("req", None), P(), P(None, ("req", "tp")), P("req"), P("req"), P("req")),
        out_specs=(P("req"), P("req"), P()),
        check_vma=False,
    )
```

profile of v0, /device:TPU:1, one launch (start us, length us, event | category | flops | bytes accessed | tf_op | source)
XLA Modules:
  0.0 312.4 jit_solution(14411869433341832396)
XLA Ops:
  7.2 0.0 copy-start
  7.2 0.0 all-gather.3.cloned.1.call-start
  7.2 0.8 broadcast_compare_fusion.2
  8.0 0.8 reduce-window.8
  8.9 0.8 convert_element_type.9
  9.7 0.7 add_add_fusion
  10.4 0.1 select_reduce_fusion.5
  10.5 0.2 select_reduce_fusion.1
  10.7 0.1 multiply_reduce_fusion.1
  10.9 0.7 convert_element_type.10
  11.6 0.7 fusion.1
  12.3 0.0 all-gather.3.cloned.1.call-update
  12.3 1.3 dynamic-slice
  14.3 0.1 add_dynamic-update-slice_fusion
  14.4 27.8 %all-reduce = s32[512]{0:T(512)S(1)} all-reduce(s32[512]{0:T(512)S(1)} %add_dynamic-update-slice_fusion), channel_id=1, replica_groups=mesh['req'=128,'tp'=4] {'req'}, use_global_device_ids=true, to_apply=%add | all-reduce | flops 512 | bytes 4096
  42.2 60.8 %all-gather.3.cloned.1.call-done = bf16[128,4,4096]{2,1,0:T(4,128)(2,1)} async-done(((bf16[1,4,4096]{2,1,0:T(4,128)(2,1)}), bf16[128,4,4096]{2,1,0:T(4,128)(2,1)}) %all-gather.3.cloned.1.call-update) | async-done | bytes 4194320 | tf_op jit(solution)/shard_map/all_gather | solution.py:23
  103.0 6.9 %reshape.92 = bf16[512,4096]{1,0:T(8,128)(2,1)} reshape(bf16[128,4,4096]{2,1,0:T(4,128)(2,1)} %all-gather.3.cloned.1.call-done) | data formatting | bytes 8388608
  109.9 0.0 copy-done
  109.9 3.5 %fusion.7 = (f32[512]{0:T(512)S(1)}, f32[512,256]{0,1:T(8,128)S(1)}) fusion(bf16[512,4096]{1,0:T(8,128)(2,1)} %reshape.92, bf16[4096,256]{1,0:T(8,128)(2,1)S(1)} %copy-done), kind=kOutput, calls=%fused_computation.38 | convolution fusion | flops 1073872384 | bytes 6817792 | tf_op jit(solution)/shard_map/dot_general | solution.py:27
  113.4 96.0 %pmax.7 = f32[512]{0:T(512)S(1)} all-reduce(f32[512]{0:T(512)S(1)} %get-tuple-element.19), channel_id=1, replica_groups=mesh['req'=128,'tp'=4] {'req','tp'}, use_global_device_ids=true, to_apply=%region_6.7 | all-reduce | flops 512 | bytes 4096 | tf_op jit(solution)/shard_map/pmax | solution.py:34
  209.5 0.2 fusion
  209.7 94.4 %psum.7 = f32[3,512]{1,0:T(4,128)S(1)} all-reduce(f32[3,512]{1,0:T(4,128)S(1)} %pad_maximum_fusion), channel_id=1, replica_groups=mesh['req'=128,'tp'=4] {'req','tp'}, use_global_device_ids=true, to_apply=%region_9.10 | all-reduce | flops 1536 | bytes 12288 | tf_op jit(solution)/shard_map/psum | solution.py:36
  304.1 0.6 select_reduce_fusion.2
  304.8 0.1 dynamic_slice.6
  304.8 0.1 dynamic_slice.7
  304.9 0.6 select_reduce_fusion.3
  (10 shorter events, 0.1 us)
Async XLA Ops:
  7.2 102.8 %copy-start = (bf16[4096,256]{1,0:T(8,128)(2,1)S(1)}, bf16[4096,256]{1,0:T(8,128)(2,1)}, u32[]{:S(2)}) copy-start(bf16[4096,256]{1,0:T(8,128)(2,1)} %param.8) | copy-start | bytes 6291460
  7.2 95.9 %all-gather.3.cloned.1.call-start = ((), (), s32[]{:S(2)}) async-start(), calls=%async_computation | async-start | bytes 4227072 | tf_op jit(solution)/shard_map/all_gather | solution.py:23
Sparse Core Ops, SparseCore 0:
  12.4 90.5 all-gather.2
where the time goes:
time: 313 us; the launch traced here: 312 us
  blocking collectives  218 us (70%)
  waiting for transfers between devices  60.9 us (19%)
  between operations  14.7 us (5%)
  local copies, waits for them, and re-layouts  8.34 us (3%)
  other arithmetic  6.62 us (2%)
  matrix products  3.49 us (1%)
    pmax x1, blocking collectives, local(): row_top = lax.pmax(own_top, ('req', 'tp'))  96 us
    psum x1, blocking collectives, local(): lax.psum(jnp.stack([own_total * factor, own_weighted * factor, own_picked...  94.4 us
    all_gather x1, waiting for transfers between devices, local(): rows, row_codes = lax.all_gather((normed, codes), 'req', axis=0, tiled=True)  60.8 us
    unnamed x1, blocking collectives  27.8 us
    unnamed x5, local copies, waits for them, and re-layouts  8.19 us
  transfers between devices with their start and end apart: 1, of which 1 were waited for; matrix products, arithmetic and copies ran while one was open for 0% of the time, Pallas kernels for 0%

commit v1 on v0

v1 whole, which is shorter than its diff:
```python
import jax
import jax.numpy as jnp
from jax import lax
from jax.experimental import pallas as pl
from jax.experimental.pallas import tpu as pltpu
from jax.sharding import PartitionSpec as P

SEQS = 4
SLOTS = 4
RING = 8
TP = 4
ROWS = 8
MESH = pl.DeviceIdType.MESH


def ring_distance(offset):
    return min(offset, RING - offset)


def forward_hops(length_up, offset):
    hops = []
    if offset < length_up:
        hops.append((offset + 1, 1))
    down = RING - 1 - length_up
    travelled = (RING - offset) % RING
    if (offset == 0 or offset > length_up) and travelled < down:
        hops.append(((offset - 1) % RING, -1))
    return hops


def joined(stats, lane):
    tops = jnp.max(jnp.where(lane == 0, stats, -jnp.inf), axis=-1, keepdims=True)
    top = jnp.max(tops, axis=0, keepdims=True)
    factor = jnp.where(lane == 3, 1.0, jnp.exp(tops - top))
    sums = jnp.sum(stats * factor, axis=0)
    return jnp.where(lane[0] == 0, top[0], sums)


def kernel(
    targets_ref, segments_ref, scored_ref, hidden_ref, gain_ref, head_ref,
    out_ref,
    rows, heads, stats, inbox_a, joined_a, inbox_b, inbox_x, parts_a, parts_b, sum_b, other_part,
    row_send, row_recv, head_sem, misc_send, misc_recv,
):
    depth, width = head_ref.shape
    req, tp = lax.axis_index("req"), lax.axis_index("tp")
    core = req % 2
    first = (req // 2) % RING
    second = req // (2 * RING)
    pos_a = first + core * (second - first)
    pos_b = second + core * (first - second)
    stride_a = 2 + core * (2 * RING - 2)
    stride_b = 2 * RING - core * (2 * RING - 2)

    def along_a(offset):
        return (req + ((pos_a + offset + RING) % RING - pos_a) * stride_a, tp)

    def along_b(offset):
        return (req + ((pos_b + offset + RING) % RING - pos_b) * stride_b, tp)

    def along_x(offset):
        return (req, (tp + offset) % TP)

    partner = (req + 1 - 2 * core, tp)

    def remote(source, target, send_sem, recv_sem, device):
        return pltpu.make_async_remote_copy(
            src_ref=source, dst_ref=target, send_sem=send_sem, recv_sem=recv_sem,
            device_id=device, device_id_type=MESH,
        )

    barrier = pltpu.get_barrier_semaphore()
    greeted = [along_a(1), along_a(-1), along_b(1), along_b(-1), partner] + [along_x(d) for d in (1, 2, 3)]
    for device in greeted:
        pl.semaphore_signal(barrier, inc=1, device_id=device, device_id_type=MESH)

    own_head = pltpu.make_async_copy(head_ref, heads.at[0], head_sem.at[0])
    own_head.start()

    slot_of, taken = [], 0
    for r in range(ROWS):
        flag = scored_ref[r]
        slot_of.append(flag * (taken + 1) - 1)
        taken = taken + flag
    hidden = hidden_ref[...].astype(jnp.float32)
    slot_row = lax.broadcasted_iota(jnp.int32, (SLOTS, depth), 0)
    values = jnp.zeros((SLOTS, depth), jnp.float32)
    slot_id = lax.broadcasted_iota(jnp.int32, (SLOTS, 128), 0)
    lane_id = lax.broadcasted_iota(jnp.int32, (SLOTS, 128), 1)
    ids = jnp.zeros((SLOTS, 128), jnp.int32)
    for r in range(ROWS):
        values = jnp.where(slot_row == slot_of[r], hidden[r : r + 1, :], values)
        ids = jnp.where(slot_id == slot_of[r], targets_ref[r], ids)
    row_scale = lax.rsqrt(jnp.mean(values * values, axis=1, keepdims=True) + 1e-05)
    normed = (values * row_scale * gain_ref[...].astype(jnp.float32)).astype(jnp.bfloat16)
    digits = jnp.where(
        lane_id == 0, ids & 63, jnp.where(lane_id == 1, (ids >> 6) & 63, jnp.where(lane_id == 2, ids >> 12, 0))
    )
    rows[0, :, :depth] = normed
    rows[0, :, depth:] = digits.astype(jnp.float32).astype(jnp.bfloat16)

    pl.semaphore_wait(barrier, len(greeted))

    def row_copy(source, target, device):
        return remote(rows.at[source], rows.at[target], row_send, row_recv.at[target], device)

    def up_length(i):
        return 4 - i % 2

    events = sorted(
        ((i, j) for i in range(RING) for j in range(RING)),
        key=lambda e: (
            ring_distance(e[0]) + (e[1] if e[1] <= up_length(e[0]) else RING - e[1]),
            e[1] != 0,
            ring_distance(e[1]),
        ),
    )
    head_copy = remote(head_ref, heads.at[1], head_sem.at[1], head_sem.at[2], partner)
    for i, j in events:
        slot = i * RING + j
        if slot:
            row_copy(slot, slot, along_b(1)).wait_recv()
        if j == 0:
            for nxt, step in forward_hops(4, i):
                row_copy(slot, nxt * RING, along_a(step)).start()
        for nxt, step in forward_hops(up_length(i), j):
            row_copy(slot, i * RING + nxt, along_b(step)).start()
        if slot == 0:
            head_copy.start()
    own_head.wait()
    head_copy.wait()

    count = RING * RING * SLOTS
    block = rows[...]
    gathered = block[:, :, :depth].reshape(count, depth)
    digit = block[:, :, depth:].astype(jnp.float32).reshape(count, 128)
    lane = lax.broadcasted_iota(jnp.int32, (count, 128), 1)
    worth = jnp.where(lane == 0, 1.0, jnp.where(lane == 1, 64.0, jnp.where(lane == 2, 4096.0, 0.0)))
    row_target = jnp.sum(digit * worth, axis=1, keepdims=True).astype(jnp.int32)
    logits = [jnp.dot(gathered, heads[h], preferred_element_type=jnp.float32) for h in range(2)]
    top = jnp.maximum(
        jnp.max(logits[0], axis=1, keepdims=True), jnp.max(logits[1], axis=1, keepdims=True)
    )
    total = weighted = picked = 0.0
    for h in range(2):
        holder = req + h * (1 - 2 * core)
        column = lax.broadcasted_iota(jnp.int32, (count, width), 1) + (holder * TP + tp) * width
        scaled = jnp.exp(logits[h] - top)
        total = total + jnp.sum(scaled, axis=1, keepdims=True)
        weighted = weighted + jnp.sum(scaled * logits[h], axis=1, keepdims=True)
        picked = picked + jnp.sum(jnp.where(column == row_target, logits[h], 0.0), axis=1, keepdims=True)
    stat = jnp.where(lane == 0, top, jnp.where(lane == 1, total, jnp.where(lane == 2, weighted, picked)))
    stats[...] = stat.reshape(RING, RING, SLOTS, 128)

    sends = []

    def exchange(pairs, send_sem, recv_sem):
        copies = [
            remote(source, target, send_sem.at[n], recv_sem.at[n], device)
            for n, (source, target, device) in enumerate(pairs)
        ]
        for copy in copies:
            copy.start()
        return copies

    def finish(copies):
        for copy in copies:
            copy.wait_recv()
        sends.extend(copies)

    copies = exchange(
        [(stats.at[i], inbox_a.at[i], along_a(-i)) for i in range(1, RING)], misc_send.at[0], misc_recv.at[0]
    )
    inbox_a[0] = stats[0]
    finish(copies)
    lane4 = lax.broadcasted_iota(jnp.int32, (1, RING, SLOTS, 128), 3)
    joined_a[...] = joined(inbox_a[...], lane4)
    copies = exchange(
        [(joined_a.at[j], inbox_b.at[j], along_b(-j)) for j in range(1, RING)], misc_send.at[1], misc_recv.at[1]
    )
    inbox_b[0] = joined_a[0]
    finish(copies)
    lane3 = lax.broadcasted_iota(jnp.int32, (1, SLOTS, 128), 2)
    inbox_x[tp] = joined(inbox_b[...], lane3)
    copies = exchange(
        [(inbox_x.at[tp], inbox_x.at[tp], along_x(d)) for d in range(1, TP)], misc_send.at[2], misc_recv.at[2]
    )
    finish(copies)
    full = joined(inbox_x[...], lane3)

    def member(n):
        return jnp.sum(jnp.where(lane_id == n, full, 0.0), axis=1, keepdims=True)

    log_norm = member(0) + jnp.log(member(1))
    logprob = member(3) - log_norm
    entropy = log_norm - member(2) / member(1)
    row_slot = jnp.full((SLOTS, 128), -1, jnp.int32)
    row_segment = jnp.full((1, 128), -1, jnp.int32)
    lane1 = lax.broadcasted_iota(jnp.int32, (1, 128), 1)
    for r in range(ROWS):
        row_slot = jnp.where(lane_id == r, slot_of[r], row_slot)
        row_segment = jnp.where(lane1 == r, segments_ref[r], row_segment)
    token_logprob = jnp.sum(jnp.where(row_slot == slot_id, logprob, 0.0), axis=0, keepdims=True)
    token_entropy = jnp.sum(jnp.where(row_slot == slot_id, entropy, 0.0), axis=0, keepdims=True)
    part = jnp.zeros((1, 128), jnp.float32)
    for s in range(SEQS):
        amount = jnp.sum(jnp.where(row_segment == s, token_logprob, 0.0), axis=1, keepdims=True)
        part = jnp.where(lane1 == s, amount, part)

    parts_a[pos_a] = part
    finish(
        exchange(
            [(parts_a.at[pos_a], parts_a.at[pos_a], along_a(i)) for i in range(1, RING)],
            misc_send.at[3], misc_recv.at[3],
        )
    )
    parts_b[pos_b] = jnp.sum(parts_a[...], axis=0)
    finish(
        exchange(
            [(parts_b.at[pos_b], parts_b.at[pos_b], along_b(j)) for j in range(1, RING)],
            misc_send.at[4], misc_recv.at[4],
        )
    )
    sum_b[...] = jnp.sum(parts_b[...], axis=0)
    finish(exchange([(sum_b, other_part, partner)], misc_send.at[5], misc_recv.at[5]))
    seq_logprob = sum_b[...] + other_part[...]
    out_ref[0:1, :] = token_logprob
    out_ref[1:2, :] = token_entropy
    out_ref[2:3, :] = seq_logprob

    for copy in sends:
        copy.wait_send()
    everything = rows.at[pl.ds(0, RING * RING - 1)]
    remote(everything, everything, row_send, row_recv.at[0], partner).wait_send()


def local(hidden, norm_gain, lm_head, targets, segments, scored):
    depth, width = lm_head.shape
    row_width = depth + 128
    smem = pl.BlockSpec(memory_space=pltpu.SMEM)
    vmem = pl.BlockSpec(memory_space=pltpu.VMEM)
    result = pl.pallas_call(
        kernel,
        out_shape=jax.ShapeDtypeStruct((8, 128), jnp.float32),
        in_specs=[smem, smem, smem, vmem, vmem, pl.BlockSpec(memory_space=pl.ANY)],
        out_specs=vmem,
        scratch_shapes=[
            pltpu.VMEM((RING * RING, SLOTS, row_width), jnp.bfloat16),
            pltpu.VMEM((2, depth, width), jnp.bfloat16),
            pltpu.VMEM((RING, RING, SLOTS, 128), jnp.float32),
            pltpu.VMEM((RING, RING, SLOTS, 128), jnp.float32),
            pltpu.VMEM((RING, SLOTS, 128), jnp.float32),
            pltpu.VMEM((RING, SLOTS, 128), jnp.float32),
            pltpu.VMEM((TP, SLOTS, 128), jnp.float32),
            pltpu.VMEM((RING, 1, 128), jnp.float32),
            pltpu.VMEM((RING, 1, 128), jnp.float32),
            pltpu.VMEM((1, 128), jnp.float32),
            pltpu.VMEM((1, 128), jnp.float32),
            pltpu.SemaphoreType.DMA,
            pltpu.SemaphoreType.DMA((RING * RING,)),
            pltpu.SemaphoreType.DMA((3,)),
            pltpu.SemaphoreType.DMA((6, RING)),
            pltpu.SemaphoreType.DMA((6, RING)),
        ],
        compiler_params=pltpu.CompilerParams(
            collective_id=0, has_side_effects=True, vmem_limit_bytes=56 * 1024 * 1024
        ),
    )(targets, segments, scored, hidden, norm_gain.reshape(1, depth), lm_head)
    return (result[0, :ROWS], result[1, :ROWS], result[2, :SEQS])


def solution(mesh):
    return jax.shard_map(
        local,
        mesh=mesh,
        in_specs=(P("req", None), P(), P(None, ("req", "tp")), P("req"), P("req"), P("req")),
        out_specs=(P("req"), P("req"), P()),
        check_vma=False,
    )
```

time: 313 us -> 73 us (0.23)
  blocking collectives: 218 us -> 0 us
  Pallas kernels: 0 us -> 68.4 us
  waiting for transfers between devices: 60.9 us -> 0 us
  between operations: 14.7 us -> 0.64 us
  other arithmetic: 6.62 us -> 0 us
  local copies, waits for them, and re-layouts: 8.34 us -> 3.75 us
  matrix products: 3.49 us -> 0 us
    pmax x1 -> x0, blocking collectives: 96 us -> none  [local(): row_top = lax.pmax(own_top, ('req', 'tp'))]
    psum x1 -> x0, blocking collectives: 94.4 us -> none  [local(): lax.psum(jnp.stack([own_total * factor, own_weighted * factor, own_picked...]
    pallas_call x0 -> x1, Pallas kernels: none -> 68.4 us  [local(): pl.pallas_call(kernel, out_shape=jax.ShapeDtypeStruct((8, 128), jnp.float...]
    all_gather x1 -> x0, waiting for transfers between devices: 60.8 us -> none  [local(): rows, row_codes = lax.all_gather((normed, codes), 'req', axis=0, tiled=True)]
    unnamed x1 -> x0, blocking collectives: 27.8 us -> none
    unnamed x5 -> x0, local copies, waits for them, and re-layouts: 8.19 us -> none
    dot_general x1 -> x0, matrix products: 3.49 us -> none  [local(): logits = jnp.dot(rows, lm_head, preferred_element_type=jnp.float32)]
  transfers between devices with their start and end apart: 1 -> 0, of which waited for: 1 -> 0; matrix products, arithmetic and copies ran while one was open for 0% -> 0% of each run, Pallas kernels for 0% -> 0%
where the time goes in v1:
time: 73 us; the launch traced here: 72.8 us
  Pallas kernels  68.4 us (94%)
  local copies, waits for them, and re-layouts  3.75 us (5%)
    pallas_call x1, Pallas kernels, local(): pl.pallas_call(kernel, out_shape=jax.ShapeDtypeStruct((8, 128), jnp.float...  68.4 us
    squeeze x2, local copies, waits for them, and re-layouts, local(): return (result[0, :ROWS], result[1, :ROWS], result[2, :SEQS])  2.45 us

profile of v1, /device:TPU:1, one launch (start us, length us, event | category | flops | bytes accessed | tf_op | source)
XLA Modules:
  0.0 72.8 jit_solution(7069012151231528707)
XLA Ops:
  0.6 1.3 %reshape.9.gain_ref = bf16[1,4096]{1,0:T(2,128)(2,1)} reshape(bf16[4096]{0:T(1024)(128)(2,1)} %param.7) | data formatting | bytes 16384 | tf_op jit(solution)/shard_map/reshape | solution.py:268
  1.9 68.4 %shard_map.85 = f32[8,128]{1,0:T(8,128)} custom-call(s32[8]{0:T(128)} %targets_ref.1, s32[8]{0:T(128)} %segments_ref.1, s32[8]{0:T(128)} %scored_ref.1, bf16[8,4096]{1,0:T(8,128)(2,1)} %hidden_ref.1, bf16[1,4096]{1,0:T(2,128)(2,1)} %reshape.9.gain_ref, bf16[4096,256]{1,0:T(8,128)(2,1)} %head_ref.1), custom_call_target="tpu_custom_call" | custom-call | tf_op jit(solution)/shard_map/pallas_call | solution.py:242
  70.3 1.2 %slice_bitcast_fusion = f32[4]{0:T(128)} fusion(f32[8,128]{1,0:T(8,128)} %shard_map.85), kind=kLoop, calls=%fused_computation | loop fusion | bytes 32 | tf_op jit(solution)/shard_map/squeeze | solution.py:269
  71.5 1.3 %slice_bitcast_fusion.1 = (f32[8]{0:T(128)}, f32[8]{0:T(128)}) fusion(f32[8,128]{1,0:T(8,128)} %shard_map.85), kind=kLoop, calls=%fused_computation.1 | loop fusion | bytes 128 | tf_op jit(solution)/shard_map/squeeze | solution.py:269

commit v2 on v1

--- a/solution.py
+++ b/solution.py
@@ -11,21 +11,7 @@
 TP = 4
 ROWS = 8
 MESH = pl.DeviceIdType.MESH
-
-
-def ring_distance(offset):
-    return min(offset, RING - offset)
-
-
-def forward_hops(length_up, offset):
-    hops = []
-    if offset < length_up:
-        hops.append((offset + 1, 1))
-    down = RING - 1 - length_up
-    travelled = (RING - offset) % RING
-    if (offset == 0 or offset > length_up) and travelled < down:
-        hops.append(((offset - 1) % RING, -1))
-    return hops
+ORDER = (0, 1, 7, 2, 6, 3, 5, 4)
 
 
 def joined(stats, lane):
@@ -39,7 +25,7 @@
 def kernel(
     targets_ref, segments_ref, scored_ref, hidden_ref, gain_ref, head_ref,
     out_ref,
-    rows, heads, stats, inbox_a, joined_a, inbox_b, inbox_x, parts_a, parts_b, sum_b, other_part,
+    rows, heads, stats, inbox_a, joined_a, inbox_b, parts_a, parts_b,
     row_send, row_recv, head_sem, misc_send, misc_recv,
 ):
     depth, width = head_ref.shape
@@ -61,7 +47,13 @@
     def along_x(offset):
         return (req, (tp + offset) % TP)
 
-    partner = (req + 1 - 2 * core, tp)
+    def shifted(device, offset):
+        return (device[0], (tp + offset) % TP)
+
+    def across(device):
+        return (device[0] + 1 - 2 * core, device[1])
+
+    partner = across((req, tp))
 
     def remote(source, target, send_sem, recv_sem, device):
         return pltpu.make_async_remote_copy(
@@ -70,7 +62,8 @@
         )
 
     barrier = pltpu.get_barrier_semaphore()
-    greeted = [along_a(1), along_a(-1), along_b(1), along_b(-1), partner] + [along_x(d) for d in (1, 2, 3)]
+    greeted = [along_a(ORDER[p]) for p in range(RING - 1, 0, -1)] + [along_b(j) for j in (2, -2, 1, -1)]
+    greeted += [along_x(d) for d in (2, 1, 3)] + [partner]
     for device in greeted:
         pl.semaphore_signal(barrier, inc=1, device_id=device, device_id_type=MESH)
 
@@ -92,7 +85,9 @@
         values = jnp.where(slot_row == slot_of[r], hidden[r : r + 1, :], values)
         ids = jnp.where(slot_id == slot_of[r], targets_ref[r], ids)
     row_scale = lax.rsqrt(jnp.mean(values * values, axis=1, keepdims=True) + 1e-05)
-    normed = (values * row_scale * gain_ref[...].astype(jnp.float32)).astype(jnp.bfloat16)
+    gain = gain_ref[...].astype(jnp.float32)
+    gain = jnp.concatenate([gain[k : k + 1, :] for k in range(depth // 128)], axis=1)
+    normed = (values * row_scale * gain).astype(jnp.bfloat16)
     digits = jnp.where(
         lane_id == 0, ids & 63, jnp.where(lane_id == 1, (ids >> 6) & 63, jnp.where(lane_id == 2, ids >> 12, 0))
     )
@@ -104,29 +99,29 @@
     def row_copy(source, target, device):
         return remote(rows.at[source], rows.at[target], row_send, row_recv.at[target], device)
 
-    def up_length(i):
-        return 4 - i % 2
-
-    events = sorted(
-        ((i, j) for i in range(RING) for j in range(RING)),
-        key=lambda e: (
-            ring_distance(e[0]) + (e[1] if e[1] <= up_length(e[0]) else RING - e[1]),
-            e[1] != 0,
-            ring_distance(e[1]),
-        ),
-    )
+    def arrived(slot):
+        row_copy(slot, slot, along_b(1)).wait_recv()
+
+    for p in range(1, RING):
+        row_copy(0, p, along_a(ORDER[p])).start()
     head_copy = remote(head_ref, heads.at[1], head_sem.at[1], head_sem.at[2], partner)
-    for i, j in events:
-        slot = i * RING + j
-        if slot:
-            row_copy(slot, slot, along_b(1)).wait_recv()
-        if j == 0:
-            for nxt, step in forward_hops(4, i):
-                row_copy(slot, nxt * RING, along_a(step)).start()
-        for nxt, step in forward_hops(up_length(i), j):
-            row_copy(slot, i * RING + nxt, along_b(step)).start()
-        if slot == 0:
+    for p in range(RING):
+        if p:
+            arrived(p)
+        for step in (2, -2, 1, -1):
+            row_copy(p, (step % RING) * RING + p, along_b(step)).start()
+        if p == 0:
             head_copy.start()
+    for p in range(RING):
+        for side in (1, -1):
+            slot = (2 * side) % RING * RING + p
+            arrived(slot)
+            if side == (1 if p % 2 else -1):
+                row_copy(slot, 4 * RING + p, along_b(2 * side)).start()
+            row_copy(slot, (3 * side) % RING * RING + p, along_b(side)).start()
+    for j in (1, 7, 3, 5, 4):
+        for p in range(RING):
+            arrived(j * RING + p)
     own_head.wait()
     head_copy.wait()
 
@@ -154,9 +149,9 @@
 
     sends = []
 
-    def exchange(pairs, send_sem, recv_sem):
+    def exchange(pairs, phase):
         copies = [
-            remote(source, target, send_sem.at[n], recv_sem.at[n], device)
+            remote(source, target, misc_send.at[phase, n], misc_recv.at[phase, n], device)
             for n, (source, target, device) in enumerate(pairs)
         ]
         for copy in copies:
@@ -169,24 +164,25 @@
         sends.extend(copies)
 
     copies = exchange(
-        [(stats.at[i], inbox_a.at[i], along_a(-i)) for i in range(1, RING)], misc_send.at[0], misc_recv.at[0]
-    )
-    inbox_a[0] = stats[0]
+        [(stats.at[:, p], inbox_a.at[p], along_a(-ORDER[p])) for p in range(RING - 1, 0, -1)], 0
+    )
+    inbox_a[0] = stats[:, 0]
     finish(copies)
     lane4 = lax.broadcasted_iota(jnp.int32, (1, RING, SLOTS, 128), 3)
     joined_a[...] = joined(inbox_a[...], lane4)
     copies = exchange(
-        [(joined_a.at[j], inbox_b.at[j], along_b(-j)) for j in range(1, RING)], misc_send.at[1], misc_recv.at[1]
-    )
-    inbox_b[0] = joined_a[0]
+        [
+            (joined_a.at[j], inbox_b.at[tp, j], shifted(along_b(-j), d))
+            for j in (4, 3, 5, 2, 6, 1, 7, 0)
+            for d in (2, 1, 3, 0)
+            if j or d
+        ],
+        1,
+    )
+    inbox_b[tp, 0] = joined_a[0]
     finish(copies)
     lane3 = lax.broadcasted_iota(jnp.int32, (1, SLOTS, 128), 2)
-    inbox_x[tp] = joined(inbox_b[...], lane3)
-    copies = exchange(
-        [(inbox_x.at[tp], inbox_x.at[tp], along_x(d)) for d in range(1, TP)], misc_send.at[2], misc_recv.at[2]
-    )
-    finish(copies)
-    full = joined(inbox_x[...], lane3)
+    full = joined(inbox_b[...].reshape(TP * RING, SLOTS, 128), lane3)
 
     def member(n):
         return jnp.sum(jnp.where(lane_id == n, full, 0.0), axis=1, keepdims=True)
@@ -208,22 +204,21 @@
         part = jnp.where(lane1 == s, amount, part)
 
     parts_a[pos_a] = part
+    finish(exchange([(parts_a.at[pos_a], parts_a.at[pos_a], along_a(ORDER[p])) for p in range(RING - 1, 0, -1)], 2))
+    parts_b[core, pos_b] = jnp.sum(parts_a[...], axis=0)
+    mine = parts_b.at[core, pos_b]
     finish(
         exchange(
-            [(parts_a.at[pos_a], parts_a.at[pos_a], along_a(i)) for i in range(1, RING)],
-            misc_send.at[3], misc_recv.at[3],
+            [
+                (mine, mine, other)
+                for p in range(RING - 1, -1, -1)
+                for other in (along_b(ORDER[p]), across(along_b(ORDER[p])))
+            ][:-2]
+            + [(mine, mine, partner)],
+            3,
         )
     )
-    parts_b[pos_b] = jnp.sum(parts_a[...], axis=0)
-    finish(
-        exchange(
-            [(parts_b.at[pos_b], parts_b.at[pos_b], along_b(j)) for j in range(1, RING)],
-            misc_send.at[4], misc_recv.at[4],
-        )
-    )
-    sum_b[...] = jnp.sum(parts_b[...], axis=0)
-    finish(exchange([(sum_b, other_part, partner)], misc_send.at[5], misc_recv.at[5]))
-    seq_logprob = sum_b[...] + other_part[...]
+    seq_logprob = jnp.sum(parts_b[...].reshape(2 * RING, 1, 128), axis=0)
     out_ref[0:1, :] = token_logprob
     out_ref[1:2, :] = token_entropy
     out_ref[2:3, :] = seq_logprob
@@ -232,6 +227,12 @@
         copy.wait_send()
     everything = rows.at[pl.ds(0, RING * RING - 1)]
     remote(everything, everything, row_send, row_recv.at[0], partner).wait_send()
+
+
+def split_kernel(result_ref, logprob_ref, entropy_ref, seq_ref):
+    logprob_ref[...] = result_ref[0, :ROWS]
+    entropy_ref[...] = result_ref[1, :ROWS]
+    seq_ref[...] = result_ref[2, :SEQS]
 
 
 def local(hidden, norm_gain, lm_head, targets, segments, scored):
@@ -250,23 +251,25 @@
             pltpu.VMEM((RING, RING, SLOTS, 128), jnp.float32),
             pltpu.VMEM((RING, RING, SLOTS, 128), jnp.float32),
             pltpu.VMEM((RING, SLOTS, 128), jnp.float32),
-            pltpu.VMEM((RING, SLOTS, 128), jnp.float32),
-            pltpu.VMEM((TP, SLOTS, 128), jnp.float32),
+            pltpu.VMEM((TP, RING, SLOTS, 128), jnp.float32),
             pltpu.VMEM((RING, 1, 128), jnp.float32),
-            pltpu.VMEM((RING, 1, 128), jnp.float32),
-            pltpu.VMEM((1, 128), jnp.float32),
-            pltpu.VMEM((1, 128), jnp.float32),
+            pltpu.VMEM((2, RING, 1, 128), jnp.float32),
             pltpu.SemaphoreType.DMA,
             pltpu.SemaphoreType.DMA((RING * RING,)),
             pltpu.SemaphoreType.DMA((3,)),
-            pltpu.SemaphoreType.DMA((6, RING)),
-            pltpu.SemaphoreType.DMA((6, RING)),
+            pltpu.SemaphoreType.DMA((4, TP * RING)),
+            pltpu.SemaphoreType.DMA((4, TP * RING)),
         ],
         compiler_params=pltpu.CompilerParams(
             collective_id=0, has_side_effects=True, vmem_limit_bytes=56 * 1024 * 1024
         ),
-    )(targets, segments, scored, hidden, norm_gain.reshape(1, depth), lm_head)
-    return (result[0, :ROWS], result[1, :ROWS], result[2, :SEQS])
+    )(targets, segments, scored, hidden, norm_gain.reshape(depth // 128, 128), lm_head)
+    return pl.pallas_call(
+        split_kernel,
+        out_shape=[jax.ShapeDtypeStruct((n,), jnp.float32) for n in (ROWS, ROWS, SEQS)],
+        in_specs=[vmem],
+        out_specs=[vmem, vmem, vmem],
+    )(result)
 
 
 def solution(mesh):

time: 73 us -> 63 us (0.86)
  Pallas kernels: 68.4 us -> 62.1 us
  local copies, waits for them, and re-layouts: 3.75 us -> 0 us
    pallas_call x1, Pallas kernels: 68.4 us -> 60.9 us  [local(): pl.pallas_call(kernel, out_shape=jax.ShapeDtypeStruct((8, 128), jnp.float...]
    squeeze x2 -> x0, local copies, waits for them, and re-layouts: 2.45 us -> none  [local(): return (result[0, :ROWS], result[1, :ROWS], result[2, :SEQS])]
    reshape x1 -> x0, local copies, waits for them, and re-layouts: 1.31 us -> none  [local(): norm_gain.reshape(1, depth)]
    pallas_call x0 -> x1, Pallas kernels: none -> 1.2 us  [local(): pl.pallas_call(split_kernel, out_shape=[jax.ShapeDtypeStruct((n,), jnp.fl...]
where the time goes in v2:
time: 63 us; the launch traced here: 62.8 us
  Pallas kernels  62.1 us (99%)
  between operations  0.64 us (1%)
    pallas_call x1, Pallas kernels, local(): pl.pallas_call(kernel, out_shape=jax.ShapeDtypeStruct((8, 128), jnp.float...  60.9 us

profile of v2, /device:TPU:1, one launch (start us, length us, event | category | flops | bytes accessed | tf_op | source)
XLA Modules:
  0.0 62.8 jit_solution(9637573694279661506)
XLA Ops:
  0.6 60.9 %shard_map.85.result_ref = f32[8,128]{1,0:T(8,128)} custom-call(s32[8]{0:T(128)} %targets_ref.1, s32[8]{0:T(128)} %segments_ref.1, s32[8]{0:T(128)} %scored_ref.1, bf16[8,4096]{1,0:T(8,128)(2,1)} %hidden_ref.1, bf16[32,128]{1,0:T(8,128)(2,1)} %bitcast.1, bf16[4096,256]{1,0:T(8,128)(2,1)} %head_ref.1), custom_call_target="tpu_custom_call" | custom-call | tf_op jit(solution)/shard_map/pallas_call | solution.py:243
  61.6 1.2 %shard_map.86 = (f32[8]{0:T(128)}, f32[8]{0:T(128)}, f32[4]{0:T(128)}) custom-call(f32[8,128]{1,0:T(8,128)} %shard_map.85.result_ref), custom_call_target="tpu_custom_call" | custom-call | tf_op jit(solution)/shard_map/pallas_call | solution.py:267

commit v3 on v2

--- a/solution.py
+++ b/solution.py
@@ -10,22 +10,23 @@
 RING = 8
 TP = 4
 ROWS = 8
+GROUP = SLOTS * RING
 MESH = pl.DeviceIdType.MESH
 ORDER = (0, 1, 7, 2, 6, 3, 5, 4)
 
 
-def joined(stats, lane):
-    tops = jnp.max(jnp.where(lane == 0, stats, -jnp.inf), axis=-1, keepdims=True)
-    top = jnp.max(tops, axis=0, keepdims=True)
-    factor = jnp.where(lane == 3, 1.0, jnp.exp(tops - top))
-    sums = jnp.sum(stats * factor, axis=0)
-    return jnp.where(lane[0] == 0, top[0], sums)
+def joined(stats):
+    tops, sums = stats[..., 0:1, :], stats[..., 1:2, :]
+    top = jnp.max(tops, axis=0)
+    lane = lax.broadcasted_iota(jnp.int32, tops.shape, tops.ndim - 1)
+    factor = jnp.where(lane >= 2 * GROUP, 1.0, jnp.exp(tops - top))
+    return top, jnp.sum(sums * factor, axis=0)
 
 
 def kernel(
     targets_ref, segments_ref, scored_ref, hidden_ref, gain_ref, head_ref,
     out_ref,
-    rows, heads, stats, inbox_a, joined_a, inbox_b, parts_a, parts_b,
+    rows, heads, stats, inbox_a, inbox_b, parts,
     row_send, row_recv, head_sem, misc_send, misc_recv,
 ):
     depth, width = head_ref.shape
@@ -81,9 +82,11 @@
     slot_id = lax.broadcasted_iota(jnp.int32, (SLOTS, 128), 0)
     lane_id = lax.broadcasted_iota(jnp.int32, (SLOTS, 128), 1)
     ids = jnp.zeros((SLOTS, 128), jnp.int32)
+    codes = jnp.zeros((SLOTS, 128), jnp.int32)
     for r in range(ROWS):
         values = jnp.where(slot_row == slot_of[r], hidden[r : r + 1, :], values)
         ids = jnp.where(slot_id == slot_of[r], targets_ref[r], ids)
+        codes = jnp.where(slot_id == slot_of[r], segments_ref[r] + 1, codes)
     row_scale = lax.rsqrt(jnp.mean(values * values, axis=1, keepdims=True) + 1e-05)
     gain = gain_ref[...].astype(jnp.float32)
     gain = jnp.concatenate([gain[k : k + 1, :] for k in range(depth // 128)], axis=1)
@@ -144,8 +147,20 @@
         total = total + jnp.sum(scaled, axis=1, keepdims=True)
         weighted = weighted + jnp.sum(scaled * logits[h], axis=1, keepdims=True)
         picked = picked + jnp.sum(jnp.where(column == row_target, logits[h], 0.0), axis=1, keepdims=True)
-    stat = jnp.where(lane == 0, top, jnp.where(lane == 1, total, jnp.where(lane == 2, weighted, picked)))
-    stats[...] = stat.reshape(RING, RING, SLOTS, 128)
+    row = lax.broadcasted_iota(jnp.int32, (count, 128), 0)
+    owner_b = (pos_b + RING - row // GROUP) % RING
+    own_lane = lane % GROUP == owner_b * SLOTS + row % SLOTS
+    sums = jnp.where(lane < GROUP, total, jnp.where(lane < 2 * GROUP, weighted, picked))
+
+    def in_lanes(value, end):
+        kept = jnp.where(own_lane & (lane < end), value, 0.0).reshape(RING, RING, SLOTS, 128)
+        return jnp.sum(jnp.sum(kept, axis=0), axis=1, keepdims=True)
+
+    code_lane = (lane_id == 3 * GROUP + pos_b * SLOTS + slot_id) & (tp == 0)
+    code = jnp.sum(jnp.where(code_lane, codes, 0).astype(jnp.float32), axis=0, keepdims=True)
+    stats[:, 0:1, :] = in_lanes(top, 2 * GROUP)
+    stats[:, 1:2, :] = in_lanes(sums, 3 * GROUP)
+    stats[0, 1:2, :] = stats[0, 1:2, :] + code
 
     sends = []
 
@@ -164,61 +179,56 @@
         sends.extend(copies)
 
     copies = exchange(
-        [(stats.at[:, p], inbox_a.at[p], along_a(-ORDER[p])) for p in range(RING - 1, 0, -1)], 0
-    )
-    inbox_a[0] = stats[:, 0]
+        [(stats.at[p], inbox_a.at[p], along_a(-ORDER[p])) for p in range(RING - 1, 0, -1)], 0
+    )
+    inbox_a[0] = stats[0]
     finish(copies)
-    lane4 = lax.broadcasted_iota(jnp.int32, (1, RING, SLOTS, 128), 3)
-    joined_a[...] = joined(inbox_a[...], lane4)
-    copies = exchange(
-        [
-            (joined_a.at[j], inbox_b.at[tp, j], shifted(along_b(-j), d))
-            for j in (4, 3, 5, 2, 6, 1, 7, 0)
-            for d in (2, 1, 3, 0)
-            if j or d
-        ],
-        1,
-    )
-    inbox_b[tp, 0] = joined_a[0]
-    finish(copies)
-    lane3 = lax.broadcasted_iota(jnp.int32, (1, SLOTS, 128), 2)
-    full = joined(inbox_b[...].reshape(TP * RING, SLOTS, 128), lane3)
-
-    def member(n):
-        return jnp.sum(jnp.where(lane_id == n, full, 0.0), axis=1, keepdims=True)
-
-    log_norm = member(0) + jnp.log(member(1))
-    logprob = member(3) - log_norm
-    entropy = log_norm - member(2) / member(1)
-    row_slot = jnp.full((SLOTS, 128), -1, jnp.int32)
-    row_segment = jnp.full((1, 128), -1, jnp.int32)
-    lane1 = lax.broadcasted_iota(jnp.int32, (1, 128), 1)
-    for r in range(ROWS):
-        row_slot = jnp.where(lane_id == r, slot_of[r], row_slot)
-        row_segment = jnp.where(lane1 == r, segments_ref[r], row_segment)
-    token_logprob = jnp.sum(jnp.where(row_slot == slot_id, logprob, 0.0), axis=0, keepdims=True)
-    token_entropy = jnp.sum(jnp.where(row_slot == slot_id, entropy, 0.0), axis=0, keepdims=True)
-    part = jnp.zeros((1, 128), jnp.float32)
-    for s in range(SEQS):
-        amount = jnp.sum(jnp.where(row_segment == s, token_logprob, 0.0), axis=1, keepdims=True)
-        part = jnp.where(lane1 == s, amount, part)
-
-    parts_a[pos_a] = part
-    finish(exchange([(parts_a.at[pos_a], parts_a.at[pos_a], along_a(ORDER[p])) for p in range(RING - 1, 0, -1)], 2))
-    parts_b[core, pos_b] = jnp.sum(parts_a[...], axis=0)
-    mine = parts_b.at[core, pos_b]
+    inbox_b[tp, pos_b, 0:1, :], inbox_b[tp, pos_b, 1:2, :] = joined(inbox_a[...])
+    mine = inbox_b.at[tp, pos_b]
     finish(
         exchange(
             [
-                (mine, mine, other)
-                for p in range(RING - 1, -1, -1)
-                for other in (along_b(ORDER[p]), across(along_b(ORDER[p])))
-            ][:-2]
-            + [(mine, mine, partner)],
-            3,
+                (mine, mine, shifted(along_b(j), d))
+                for j in (4, 3, 5, 2, 6, 1, 7, 0)
+                for d in (2, 1, 3, 0)
+                if j or d
+            ],
+            1,
         )
     )
-    seq_logprob = jnp.sum(parts_b[...].reshape(2 * RING, 1, 128), axis=0)
+    full_top, full_sums = joined(inbox_b[...].reshape(TP * RING, 2, 128))
+    row_id = lax.broadcasted_iota(jnp.int32, (GROUP, 128), 0)
+    row_lane = lax.broadcasted_iota(jnp.int32, (GROUP, 128), 1)
+
+    def member(value, n):
+        return jnp.sum(jnp.where(row_lane == row_id + n * GROUP, value, 0.0), axis=1, keepdims=True)
+
+    full_total = member(full_sums, 0)
+    log_norm = member(full_top, 0) + jnp.log(full_total)
+    logprob = member(full_sums, 2) - log_norm
+    entropy = log_norm - member(full_sums, 1) / full_total
+    row_code = member(full_sums, 3).astype(jnp.int32)
+    part = jnp.sum(jnp.where(row_code == row_lane + 1, logprob, 0.0), axis=0, keepdims=True)
+
+    parts[core, pos_a] = part
+    own_sum = parts.at[core, pos_a]
+    copies = exchange(
+        [
+            (own_sum, own_sum, other)
+            for p in range(RING - 1, 0, -1)
+            for other in (along_a(ORDER[p]), across(along_a(ORDER[p])))
+        ]
+        + [(own_sum, own_sum, partner)],
+        2,
+    )
+    row_slot = jnp.full((GROUP, 128), -1, jnp.int32)
+    for r in range(ROWS):
+        row_slot = jnp.where(row_lane == r, slot_of[r], row_slot)
+    own_row = (row_slot >= 0) & (row_id == row_slot + pos_b * SLOTS)
+    token_logprob = jnp.sum(jnp.where(own_row, logprob, 0.0), axis=0, keepdims=True)
+    token_entropy = jnp.sum(jnp.where(own_row, entropy, 0.0), axis=0, keepdims=True)
+    finish(copies)
+    seq_logprob = jnp.sum(parts[...].reshape(2 * RING, 1, 128), axis=0)
     out_ref[0:1, :] = token_logprob
     out_ref[1:2, :] = token_entropy
     out_ref[2:3, :] = seq_logprob
@@ -248,17 +258,15 @@
         scratch_shapes=[
             pltpu.VMEM((RING * RING, SLOTS, row_width), jnp.bfloat16),
             pltpu.VMEM((2, depth, width), jnp.bfloat16),
-            pltpu.VMEM((RING, RING, SLOTS, 128), jnp.float32),
-            pltpu.VMEM((RING, RING, SLOTS, 128), jnp.float32),
-            pltpu.VMEM((RING, SLOTS, 128), jnp.float32),
-            pltpu.VMEM((TP, RING, SLOTS, 128), jnp.float32),
-            pltpu.VMEM((RING, 1, 128), jnp.float32),
+            pltpu.VMEM((RING, 2, 128), jnp.float32),
+            pltpu.VMEM((RING, 2, 128), jnp.float32),
+            pltpu.VMEM((TP, RING, 2, 128), jnp.float32),
             pltpu.VMEM((2, RING, 1, 128), jnp.float32),
             pltpu.SemaphoreType.DMA,
             pltpu.SemaphoreType.DMA((RING * RING,)),
             pltpu.SemaphoreType.DMA((3,)),
-            pltpu.SemaphoreType.DMA((4, TP * RING)),
-            pltpu.SemaphoreType.DMA((4, TP * RING)),
+            pltpu.SemaphoreType.DMA((3, TP * RING)),
+            pltpu.SemaphoreType.DMA((3, TP * RING)),
         ],
         compiler_params=pltpu.CompilerParams(
             collective_id=0, has_side_effects=True, vmem_limit_bytes=56 * 1024 * 1024

time: 63 us -> 57.6 us (0.914)
  Pallas kernels: 62.1 us -> 56.8 us
    pallas_call x1, Pallas kernels: 60.9 us -> 55.6 us  [local(): pl.pallas_call(kernel, out_shape=jax.ShapeDtypeStruct((8, 128), jnp.float...]
where the time goes in v3:
time: 57.6 us; the launch traced here: 57.4 us
  Pallas kernels  56.8 us (99%)
  between operations  0.64 us (1%)
    pallas_call x1, Pallas kernels, local(): pl.pallas_call(kernel, out_shape=jax.ShapeDtypeStruct((8, 128), jnp.float...  55.6 us
    pallas_call x1, Pallas kernels, local(): pl.pallas_call(split_kernel, out_shape=[jax.ShapeDtypeStruct((n,), jnp.fl...  1.2 us

profile of v3, /device:TPU:1, one launch (start us, length us, event | category | flops | bytes accessed | tf_op | source)
XLA Modules:
  0.0 57.4 jit_solution(524065850263830224)
XLA Ops:
  0.6 55.6 %shard_map.85.result_ref = f32[8,128]{1,0:T(8,128)} custom-call(s32[8]{0:T(128)} %targets_ref.1, s32[8]{0:T(128)} %segments_ref.1, s32[8]{0:T(128)} %scored_ref.1, bf16[8,4096]{1,0:T(8,128)(2,1)} %hidden_ref.1, bf16[32,128]{1,0:T(8,128)(2,1)} %bitcast.1, bf16[4096,256]{1,0:T(8,128)(2,1)} %head_ref.1), custom_call_target="tpu_custom_call" | custom-call | tf_op jit(solution)/shard_map/pallas_call | solution.py:253
  56.2 1.2 %shard_map.86 = (f32[8]{0:T(128)}, f32[8]{0:T(128)}, f32[4]{0:T(128)}) custom-call(f32[8,128]{1,0:T(8,128)} %shard_map.85.result_ref), custom_call_target="tpu_custom_call" | custom-call | tf_op jit(solution)/shard_map/pallas_call | solution.py:275

commit v4 on v3

--- a/solution.py
+++ b/solution.py
@@ -105,14 +105,19 @@
     def arrived(slot):
         row_copy(slot, slot, along_b(1)).wait_recv()
 
+    def spread(p):
+        for step in (1, -1, 2, -2):
+            row_copy(p, (step % RING) * RING + p, along_b(step)).start()
+
     for p in range(1, RING):
+        if p == 3:
+            spread(0)
         row_copy(0, p, along_a(ORDER[p])).start()
     head_copy = remote(head_ref, heads.at[1], head_sem.at[1], head_sem.at[2], partner)
     for p in range(RING):
         if p:
             arrived(p)
-        for step in (2, -2, 1, -1):
-            row_copy(p, (step % RING) * RING + p, along_b(step)).start()
+            spread(p)
         if p == 0:
             head_copy.start()
     for p in range(RING):

time: 57.6 us -> 57.7 us (level)
  no operation moved by 1% of the time
where the time goes in v4:
time: 57.7 us; the launch traced here: 57.5 us
  Pallas kernels  56.8 us (98%)
  between operations  0.64 us (1%)
    pallas_call x1, Pallas kernels, local(): pl.pallas_call(kernel, out_shape=jax.ShapeDtypeStruct((8, 128), jnp.float...  55.6 us
    pallas_call x1, Pallas kernels, local(): pl.pallas_call(split_kernel, out_shape=[jax.ShapeDtypeStruct((n,), jnp.fl...  1.2 us

profile of v4, /device:TPU:1, one launch (start us, length us, event | category | flops | bytes accessed | tf_op | source)
XLA Modules:
  0.0 57.5 jit_solution(330076585076856884)
XLA Ops:
  0.6 55.6 %shard_map.85.result_ref = f32[8,128]{1,0:T(8,128)} custom-call(s32[8]{0:T(128)} %targets_ref.1, s32[8]{0:T(128)} %segments_ref.1, s32[8]{0:T(128)} %scored_ref.1, bf16[8,4096]{1,0:T(8,128)(2,1)} %hidden_ref.1, bf16[32,128]{1,0:T(8,128)(2,1)} %bitcast.1, bf16[4096,256]{1,0:T(8,128)(2,1)} %head_ref.1), custom_call_target="tpu_custom_call" | custom-call | tf_op jit(solution)/shard_map/pallas_call | solution.py:258
  56.3 1.2 %shard_map.86 = (f32[8]{0:T(128)}, f32[8]{0:T(128)}, f32[4]{0:T(128)}) custom-call(f32[8,128]{1,0:T(8,128)} %shard_map.85.result_ref), custom_call_target="tpu_custom_call" | custom-call | tf_op jit(solution)/shard_map/pallas_call | solution.py:280
